TPU v7x, 32 devices: a whole 2x2x4 slice. The times are simulated.
32 devices in a mesh: panel: 16 (over z, x, core), freq: 2 (over y).
Axes of the slice: x: 2, y: 2, z: 4, core: 2. Of those that a mesh axis runs over, the one named last changes fastest.
Arguments:
- sources: bfloat16 [2, 4096, 1024], P(None, ('panel', 'freq')), may hold values from -6 to 6
- panel_pos: float32 [3, 4096], P(None, 'panel'), may hold values from -30 to 30
- normal_angles: float32 [2, 4096], P(None, 'panel'), may hold values from -3.140625 to 3.140625
- observer_angles: float32 [2, 2048], replicated, may hold values from -3.140625 to 3.140625
- absorption: float32 [64, 16], replicated, may hold values from 0.05 to 1
- ray_count: int32 [131072], P('panel'), may hold values from 1 to 8
- ray_layer: int32 [8, 131072], P(None, 'panel'), may hold values from 0 to 15
- ray_length: float32 [8, 131072], P(None, 'panel'), may hold values from 0.1 to 1
- ray_weight: float32 [131072], P('panel'), may hold values from 0.01 to 0.1
- ray_ground: int32 [131072], P('panel'), may hold values from 0 to 4095
Outputs:
- obs_spectrum: float32 [2048, 128], P('panel', 'freq')
- ground_power: float32 [64, 4096], P(None, 'panel')
All inputs are finite; a program needn't handle non-finite values.
Results may differ from a plain program's by a relative error of at most 0.0026.
Values may be sent and summed in bfloat16 or wider, within the bound.
A program may use at most 64 MiB of HBM per device.

v0:
```python
import functools
import math

import jax
import jax.numpy as jnp
import numpy as np
from jax import lax
from jax.experimental import pallas as pl
from jax.experimental.pallas import tpu as pltpu
from jax.sharding import PartitionSpec as P

SAMPLES = 1024
BIN0 = 32
RADIUS = 150.0
GAIN = 3.0
GROUND = 4096
REACH = 52.0
BLOCK = 16
BLOCKS = 3
ORDERS = BLOCK * BLOCKS
UNITS = BLOCK * BLOCKS * (BLOCKS + 1) // 2
TOP = 56
MESH = pl.DeviceIdType.MESH
VMEM = pltpu.MemorySpace.VMEM


def dft_rows(samples, first_bin, groups, per_group):
    index = np.arange(samples)
    bins = first_bin + np.arange(groups * per_group)
    angle = 2.0 * np.pi / samples * (bins[:, None] * index[None, :] % samples)
    window = (0.5 - 0.5 * np.cos(2.0 * np.pi / samples * index)) / math.sqrt(samples)
    rows = np.stack([window * np.cos(angle), -window * np.sin(angle)])
    rows = rows.reshape(2, groups, per_group, samples).transpose(1, 0, 2, 3)
    return rows.reshape(-1, samples).astype(np.float32)


def sincos_turns(turns):
    part = turns - jnp.round(turns)
    square = part * part
    sine = jnp.float32(-(math.pi**11) / math.factorial(11))
    for power in (9, 7, 5, 3, 1):
        sign = 1.0 if power % 4 == 1 else -1.0
        sine = sine * square + sign * math.pi**power / math.factorial(power)
    sine = sine * part
    cosine = jnp.float32(math.pi**12 / math.factorial(12))
    for power in (10, 8, 6, 4, 2, 0):
        sign = 1.0 if power % 4 == 0 else -1.0
        cosine = cosine * square + sign * math.pi**power / math.factorial(power)
    return 1.0 - 2.0 * sine * sine, 2.0 * sine * cosine


def enter(axis, count):
    barrier = pltpu.get_barrier_semaphore()
    me = lax.axis_index(axis)
    for step in range(1, count):
        pl.semaphore_signal(
            barrier, inc=1, device_id={axis: lax.rem(me + step, count)}, device_id_type=MESH
        )
    return barrier


def split_float(value):
    pieces = []
    for _ in range(3):
        pieces.append(value.astype(jnp.bfloat16))
        value = value - pieces[-1].astype(jnp.float32)
    return pieces


def unit_base(block):
    return sum(ORDERS - BLOCK * earlier for earlier in range(block))


def expansion_table(groups, freqs, weighting):
    wave = 2.0 * np.pi / SAMPLES * (BIN0 + np.arange(groups * freqs))
    reach = wave * RADIUS
    below = np.exp(-1j * reach) / reach * 1j
    hankel = [below, (1 / reach + 1j) * below]
    for n in range(1, ORDERS):
        hankel.append((2 * n + 1) / reach * hankel[n] - hankel[n - 1])
    hankel = np.stack(hankel[:ORDERS])
    radial = (RADIUS * weighting) * (-1j * wave)[None] * hankel
    rows = np.zeros((2, groups * freqs, UNITS * 2 * BLOCK))
    start = 2.0
    for m in range(ORDERS):
        if m:
            start *= 4 * m * m / (2 * m * (2 * m + 1))
        norm = start * (np.pi if m else 2 * np.pi)
        block = m // BLOCK
        for n in range(m, ORDERS):
            if n > m:
                norm *= 4 * (n * n - m * m) / (4 * n * n - 1)
            at = (unit_base(block) + n - BLOCK * block) * 2 * BLOCK + m - BLOCK * block
            value = 4 * np.pi / norm * radial[n]
            for side in range(2 if m else 1):
                rows[0, :, at + BLOCK * side] = value.real
                rows[1, :, at + BLOCK * side] = value.imag
    rows = rows.reshape(2, groups, freqs, -1).transpose(1, 0, 2, 3)
    return rows.astype(np.float32)


def times(left, right):
    return (left[0] * right[0] - left[1] * right[1], left[0] * right[1] + left[1] * right[0])


def azimuth_powers(real, imaginary, shape):
    one = (jnp.broadcast_to(real, shape), jnp.broadcast_to(imaginary, shape))
    row = lax.broadcasted_iota(jnp.int32, shape, 0)
    square = times(one, one)
    fourth = times(square, square)
    eighth = times(fourth, fourth)
    first = None
    for bit, power in ((1, one), (2, square), (4, fourth)):
        picked = (jnp.where(row & bit, power[0], 1.0), jnp.where(row & bit, power[1], 0.0))
        first = picked if first is None else times(first, picked)
    tiles = [first]
    for _ in range(ORDERS // 8 - 1):
        tiles.append(times(tiles[-1], eighth))
    seventh = times(times(fourth, square), one)
    before = [(pltpu.roll(first[0], 1, axis=0), pltpu.roll(first[1], 1, axis=0))]
    before += [times(tile, seventh) for tile in tiles[:-1]]
    return tiles, before


def join(tiles, block, part):
    per = BLOCK // 8
    return jnp.concatenate([tile[part] for tile in tiles[block * per : (block + 1) * per]], axis=0)


def radiate_kernel(freqs, panels, lanes, spectra_ref, pos_ref, normal_ref, angle_ref, table_ref,
                   out_ref, directions, basis, moments, radial, sums, mine, theirs, table, weights,
                   parts, landed, table_sem, pair_send, pair_recv, send_sem, recv_sem):
    owners = 2 * parts.shape[0]
    half = owners // 2
    me = lax.axis_index("panel")
    core = lax.rem(me, 2)
    chip = lax.div(me, 2)
    sibling = me + 1 - 2 * core
    group = lax.axis_index("freq")
    step = 2.0 * math.pi / SAMPLES
    fetch = pltpu.make_async_copy(table_ref.at[group], table, table_sem)
    fetch.start()
    barrier = enter("panel", owners)

    def pair_copy(chunk):
        at = pl.ds(pl.multiple_of(chunk * 128, 128), 128)
        return pltpu.make_async_remote_copy(
            src_ref=mine.at[:, at],
            dst_ref=theirs.at[:, at],
            send_sem=pair_send.at[chunk],
            recv_sem=pair_recv.at[chunk],
            device_id={"panel": sibling},
            device_id_type=MESH,
        )

    def transfer(source, target):
        return pltpu.make_async_remote_copy(
            src_ref=parts.at[target],
            dst_ref=landed.at[source],
            send_sem=send_sem.at[target],
            recv_sem=recv_sem.at[source],
            device_id={"panel": 2 * target + core},
            device_id_type=MESH,
        )

    for order in range(half):
        both = angle_ref[:, 2 * order * lanes : 2 * (order + 1) * lanes]
        angle = jnp.where(core == 0, both[:, 0:lanes], both[:, lanes : 2 * lanes])
        cosine, sine = sincos_turns(angle * jnp.float32(0.5 / math.pi))
        to = slice(order * lanes, (order + 1) * lanes)
        directions[0:1, to] = sine[0:1] * cosine[1:2]
        directions[1:2, to] = sine[0:1] * sine[1:2]
        directions[2:3, to] = -cosine[0:1]
    shape = (BLOCK, 128)
    row = lax.broadcasted_iota(jnp.int32, shape, 0)

    def slope(order, block):
        m = (row + BLOCK * block).astype(jnp.float32)
        return (float(order * order) - m * m) * (4.0 / (4.0 * order * order - 1.0))

    wide = 4

    def observe(index, carry):
        lane = [
            pl.ds(pl.multiple_of(index * (128 * wide) + 128 * n, 128), 128) for n in range(wide)
        ]
        powers = [
            azimuth_powers(directions[0:1, at], directions[1:2, at], (8, 128))[0] for at in lane
        ]
        double = [jnp.broadcast_to(2.0 * directions[2:3, at], shape) for at in lane]
        for block in range(BLOCKS):
            first = BLOCK * block
            cosines = [join(tiles, block, 0) for tiles in powers]
            sines = [join(tiles, block, 1) for tiles in powers]
            now = [jnp.where(row == 0, 1.0, 0.0)] * wide
            past = [jnp.zeros(shape, jnp.float32)] * wide
            for order in range(first, ORDERS):
                at_row = (unit_base(block) + order - first) * 2 * BLOCK
                for n in range(wide):
                    basis[at_row : at_row + BLOCK, lane[n]] = (now[n] * cosines[n]).astype(
                        jnp.bfloat16
                    )
                    basis[at_row + BLOCK : at_row + 2 * BLOCK, lane[n]] = (
                        now[n] * sines[n]
                    ).astype(jnp.bfloat16)
                if order + 1 < ORDERS:
                    beta = slope(order, block)
                    for n in range(wide):
                        later = double[n] * now[n] - beta * past[n]
                        if order + 1 - first < BLOCK:
                            later = jnp.where(row == order + 1 - first, 1.0, later)
                        past[n], now[n] = now[n], later
        return carry

    lax.fori_loop(0, half * lanes // (128 * wide), observe, 0)

    def emit(unit, part, at, value):
        high = value.astype(jnp.bfloat16)
        low = (value - high.astype(jnp.float32)).astype(jnp.bfloat16)
        moments[unit, part * BLOCK : (part + 1) * BLOCK, at] = high
        moments[unit, (2 + part) * BLOCK : (3 + part) * BLOCK, at] = low

    def locate(index, carry):
        at = pl.ds(pl.multiple_of(index * 128, 128), 128)
        beside = pl.ds(pl.multiple_of(panels + index * 128, 128), 128)
        place = pos_ref[:, at] * jnp.float32(1.0 / REACH)
        cosine, sine = sincos_turns(normal_ref[:, at] * jnp.float32(0.5 / math.pi))
        normal = [sine[0:1] * cosine[1:2], sine[0:1] * sine[1:2], cosine[0:1]]
        across = sum(place[n : n + 1] * normal[n] for n in range(3))
        square = sum(place[n : n + 1] * place[n : n + 1] for n in range(3))
        tiles, before = azimuth_powers(place[0:1], place[1:2], (8, 128))
        tilt = (jnp.broadcast_to(normal[0], (8, 128)), jnp.broadcast_to(normal[1], (8, 128)))
        turned = [times(value, tilt) for value in before]
        double = jnp.broadcast_to(2.0 * place[2:3], shape)
        lean = jnp.broadcast_to(2.0 * normal[2], shape)
        size = jnp.broadcast_to(square, shape)
        grow = jnp.broadcast_to(2.0 * across, shape)
        for block in range(BLOCKS):
            first = BLOCK * block
            cosines, sines = join(tiles, block, 0), join(tiles, block, 1)
            m = (row + first).astype(jnp.float32)
            cosines_by = join(turned, block, 0) * m
            sines_by = join(turned, block, 1) * m
            now = jnp.where(row == 0, 1.0, 0.0)
            past = rate = rate_past = jnp.zeros(shape, jnp.float32)
            for order in range(first, ORDERS):
                unit = unit_base(block) + order - first
                emit(unit, 0, at, now * cosines)
                emit(unit, 1, at, now * sines)
                emit(unit, 0, beside, rate * cosines + now * cosines_by)
                emit(unit, 1, beside, rate * sines + now * sines_by)
                if order + 1 < ORDERS:
                    beta = slope(order, block)
                    beta_size = beta * size
                    later = double * now - beta_size * past
                    rate_later = (lean * now + double * rate) - (
                        (beta * grow) * past + beta_size * rate_past
                    )
                    if order + 1 - first < BLOCK:
                        later = jnp.where(row == order + 1 - first, 1.0, later)
                    past, now = now, later
                    rate_past, rate = rate, rate_later
        return carry

    lax.fori_loop(0, panels // 128, locate, 0)
    place = pos_ref[...]
    cosine, sine = sincos_turns(normal_ref[...] * jnp.float32(0.5 / math.pi))
    across = (
        sine[0:1] * cosine[1:2] * place[0:1]
        + sine[0:1] * sine[1:2] * place[1:2]
        + cosine[0:1] * place[2:3]
    )
    square = place[0:1] * place[0:1] + place[1:2] * place[1:2] + place[2:3] * place[2:3]
    length = square * lax.rsqrt(jnp.maximum(square, 1e-30))
    bins = lax.broadcasted_iota(jnp.int32, (freqs, panels), 0) + (BIN0 + group * freqs)
    wave = bins.astype(jnp.float32) * jnp.float32(step)
    size = square * jnp.float32(1.0 / REACH**2)
    argument = wave * length
    log_start = (
        12.0 * math.log(10.0)
        - math.lgamma(2 * TOP + 3)
        + (TOP + 1) * math.log(2.0)
        + math.lgamma(TOP + 2)
    )
    kappa = wave * jnp.float32(REACH)
    inverse = 1.0 / kappa
    later = jnp.zeros((freqs, panels), jnp.float32)
    now = jnp.exp(
        TOP * jnp.log(kappa) + jnp.float32(log_start) - argument * argument / (4.0 * TOP + 6.0)
    )
    size = jnp.broadcast_to(size, (freqs, panels))
    for order in range(TOP, 0, -1):
        earlier = (float(2 * order + 1) * inverse) * now - size * later
        later, now = now, earlier
        if order - 1 <= ORDERS:
            radial[order - 1] = now
    near = later * (length * jnp.float32(1.0 / REACH))
    cosine, sine = sincos_turns(argument * jnp.float32(0.5 / math.pi))
    safe = jnp.maximum(argument, 0.05)
    over = 1.0 / safe
    small = argument < 0.05
    zero = jnp.where(small, 1.0 - argument * argument * (1.0 / 6.0), sine * over)
    one = jnp.where(small, argument * (1.0 / 3.0), (sine * over - cosine) * over)
    scale = (now * zero + near * one) / (now * now + near * near)
    heavy = scale * wave

    def both(value):
        return jnp.concatenate([value, value], axis=0)

    monopole = jnp.concatenate(
        [-heavy * spectra_ref[freqs : 2 * freqs], heavy * spectra_ref[0:freqs]], axis=0
    )
    loading = spectra_ref[2 * freqs : 4 * freqs] * both(scale)
    facing = loading * both(-wave * across * jnp.float32(1.0 / REACH))
    loading = loading * jnp.float32(1.0 / REACH)
    sums[0] = monopole
    sums[1] = facing
    sums[2] = loading
    pl.semaphore_wait(barrier, owners - 1)

    def project(blocks, quad, carry):
        values = [[] for _ in range(blocks)]
        for inner in range(4):
            order = quad * 4 + inner
            here, above = both(radial[order]), both(radial[order + 1])
            strength = jnp.concatenate(
                [sums[0] * here + sums[1] * above, sums[2] * here], axis=1
            )
            high = strength.astype(jnp.bfloat16).astype(jnp.float32)
            right = jnp.concatenate([high, strength - high], axis=0).astype(jnp.bfloat16)
            left = jnp.concatenate(
                [moments[unit_base(b) - BLOCK * b + order] for b in range(blocks)], axis=0
            )
            product = lax.dot_general(
                left, right, (((1,), (1,)), ((), ())), preferred_element_type=jnp.float32
            )
            for b in range(blocks):
                begin = 4 * BLOCK * b
                values[b].append(
                    product[begin : begin + 2 * BLOCK]
                    + product[begin + 2 * BLOCK : begin + 4 * BLOCK]
                )
        for b in range(blocks):
            turned = jnp.transpose(jnp.concatenate(values[b], axis=0))
            chunk = (unit_base(b) - BLOCK * b) // 4 + quad
            at = pl.ds(pl.multiple_of(chunk * 128, 128), 128)
            mine[:, at] = turned[0 : 2 * freqs] + turned[2 * freqs : 4 * freqs]
            pair_copy(chunk).start()
        return carry

    per = BLOCK // 4
    for section in range(BLOCKS):
        lax.fori_loop(
            section * per, (section + 1) * per, functools.partial(project, section + 1), 0
        )
    fetch.wait()

    def merge(chunk, carry):
        pair_copy(chunk).wait_recv()
        at = pl.ds(pl.multiple_of(chunk * 128, 128), 128)
        value = mine[:, at] + theirs[:, at]
        real, imaginary = value[0:freqs], value[freqs : 2 * freqs]
        by_real, by_imaginary = table[0, :, at], table[1, :, at]
        value = jnp.concatenate(
            [
                real * by_real - imaginary * by_imaginary,
                real * by_imaginary + imaginary * by_real,
            ],
            axis=0,
        )
        high = value.astype(jnp.bfloat16).astype(jnp.float32)
        weights[:, at] = jnp.concatenate([high, value - high], axis=0).astype(jnp.bfloat16)
        return carry

    lax.fori_loop(0, UNITS // 4, merge, 0)
    each = 2 if half % 2 == 0 else 1

    def field(order, carry):
        pick = lax.rem(lax.div(chip, each) + 1 + order, half // each)
        at = pl.ds(pl.multiple_of(pick * (each * lanes), each * lanes), each * lanes)
        product = jnp.dot(weights[...], basis[:, at], preferred_element_type=jnp.float32)
        product = product[0 : 2 * freqs] + product[2 * freqs : 4 * freqs]
        for side in range(each):
            target = pick * each + side
            parts[target] = product[:, side * lanes : (side + 1) * lanes]

            @pl.when(target != chip)
            def _():
                transfer(chip, target).start()

        return carry

    lax.fori_loop(0, half // each, field, 0)
    total = parts[chip]
    for n in range(1, half):
        source = lax.rem(chip + n, half)
        transfer(source, source).wait_recv()
        total = total + landed[source]
    out_ref[...] = total
    for n in range(1, half):
        target = lax.rem(chip + n, half)
        transfer(target, target).wait_send()

    def drain(chunk, carry):
        pair_copy(chunk).wait_send()
        return carry

    lax.fori_loop(0, UNITS // 4, drain, 0)


def radiate(spectra, positions, normals, angles, owners, groups, weighting):
    panels = spectra.shape[1]
    freqs = spectra.shape[0] // 4
    observers = angles.shape[1]
    lanes = observers // owners
    half = owners // 2
    depth = UNITS * 2 * BLOCK
    table = jnp.asarray(expansion_table(groups, freqs, weighting))
    return pl.pallas_call(
        functools.partial(radiate_kernel, freqs, panels, lanes),
        out_shape=jax.ShapeDtypeStruct((2 * freqs, lanes), jnp.float32),
        in_specs=[pl.BlockSpec(memory_space=VMEM)] * 4 + [pl.BlockSpec(memory_space=pl.ANY)],
        out_specs=pl.BlockSpec(memory_space=VMEM),
        scratch_shapes=[
            pltpu.VMEM((8, half * lanes), jnp.float32),
            pltpu.VMEM((depth, half * lanes), jnp.bfloat16),
            pltpu.VMEM((UNITS, 4 * BLOCK, 2 * panels), jnp.bfloat16),
            pltpu.VMEM((ORDERS + 1, freqs, panels), jnp.float32),
            pltpu.VMEM((3, 2 * freqs, panels), jnp.float32),
            pltpu.VMEM((2 * freqs, depth), jnp.float32),
            pltpu.VMEM((2 * freqs, depth), jnp.float32),
            pltpu.VMEM((2, freqs, depth), jnp.float32),
            pltpu.VMEM((4 * freqs, depth), jnp.bfloat16),
            pltpu.VMEM((half, 2 * freqs, lanes), jnp.float32),
            pltpu.VMEM((half, 2 * freqs, lanes), jnp.float32),
            pltpu.SemaphoreType.DMA,
            pltpu.SemaphoreType.DMA((UNITS // 4,)),
            pltpu.SemaphoreType.DMA((UNITS // 4,)),
            pltpu.SemaphoreType.DMA((half,)),
            pltpu.SemaphoreType.DMA((half,)),
        ],
        compiler_params=pltpu.CompilerParams(
            vmem_limit_bytes=60 * 1024 * 1024,
            collective_id=1,
            has_side_effects=True,
        ),
        name="radiate",
    )(spectra, positions, normals, angles, table)


def ground_kernel(chunk, rays, owners, groups, each, spectrum_ref, absorption_ref, count_ref,
                  layer_ref, length_ref, weight_ref, ground_ref, out_ref, spreading, energies, lows, left,
                  total, own, parts, landed, mine, others, send_sem, recv_sem, send_group,
                  recv_group):
    freqs = absorption_ref.shape[0]
    layers = absorption_ref.shape[1]
    observers = spectrum_ref.shape[1]
    low_size = out_ref.shape[1]
    me = lax.axis_index("panel")
    group = lax.axis_index("freq")
    barrier = enter("panel", owners)
    enter("freq", groups)
    real, imaginary = spectrum_ref[0:freqs, :], spectrum_ref[freqs : 2 * freqs, :]
    power = real * real + imaginary * imaginary
    chunks = count_ref.shape[1] // chunk
    split = split_float(absorption_ref[...])
    absorb = jnp.concatenate([split[i] for i in (0, 0, 1, 0, 1, 2)], axis=1)
    shape = (observers, chunk)
    begin = lax.broadcasted_iota(jnp.int32, shape, 0) * rays
    column = lax.broadcasted_iota(jnp.int32, shape, 1)
    same_owner = (column >= begin) & (column < begin + rays)
    spreading[...] = jnp.where(same_owner, 1.0, 0.0).astype(jnp.bfloat16)

    def transfer(source, target):
        return pltpu.make_async_remote_copy(
            src_ref=parts.at[target],
            dst_ref=landed.at[source],
            send_sem=send_sem.at[target],
            recv_sem=recv_sem.at[source],
            device_id={"panel": target},
            device_id_type=MESH,
        )

    def prepare(index, carry):
        at = pl.ds(pl.multiple_of(index * chunk, chunk), chunk)
        layer_ids = lax.broadcasted_iota(jnp.int32, (layers, chunk), 0)
        count = count_ref[0:1, at]
        lengths = jnp.zeros((layers, chunk), jnp.float32)
        for segment in range(layer_ref.shape[0]):
            used = jnp.where(segment < count, length_ref[segment : segment + 1, at], 0.0)
            same = layer_ref[segment : segment + 1, at] == layer_ids
            lengths = lengths + jnp.where(same, used, 0.0)
        split = split_float(lengths)
        lengths = jnp.concatenate([split[i] for i in (0, 1, 0, 2, 1, 0)], axis=0)
        depth = jnp.dot(absorb, lengths, preferred_element_type=jnp.float32)
        turned = pltpu.roll(power, lax.rem(observers - index * (chunk // rays), observers), axis=1)
        spread = jnp.dot(
            jnp.concatenate(split_float(turned), axis=0),
            spreading[...],
            preferred_element_type=jnp.float32,
        )
        spread = spread[0:freqs] + spread[freqs : 2 * freqs] + spread[2 * freqs : 3 * freqs]
        energy = spread * weight_ref[0:1, at] * jnp.exp(-depth)
        energies[:, at] = energy.astype(jnp.bfloat16)
        within = ground_ref[0:1, at] & (low_size - 1)
        ids = lax.broadcasted_iota(jnp.int32, (low_size, chunk), 0)
        lows[:, at] = jnp.where(ids == within, 1.0, 0.0).astype(jnp.bfloat16)
        return carry

    lax.fori_loop(0, chunks, prepare, 0)
    pl.semaphore_wait(barrier, owners + groups - 2)

    def batch(order, carry):
        base = lax.rem(lax.div(me, each) + 1 + order, owners // each) * each
        total[...] = jnp.zeros_like(total)

        def step(index, carry):
            at = pl.ds(pl.multiple_of(index * chunk, chunk), chunk)
            block = ground_ref[0:1, at] // low_size
            for n in range(each):
                keep = jnp.where(block == base + n, 1.0, 0.0).astype(jnp.bfloat16)
                left[n * freqs : (n + 1) * freqs, :] = energies[:, at] * keep
            total[...] += lax.dot_general(
                left[...],
                lows[:, at],
                (((1,), (1,)), ((), ())),
                preferred_element_type=jnp.float32,
            )
            return carry

        lax.fori_loop(0, chunks, step, 0)
        for n in range(each):
            target = base + n
            value = total[n * freqs : (n + 1) * freqs, :]
            parts[target] = value.astype(jnp.bfloat16)

            @pl.when(target != me)
            def _():
                transfer(me, target).start()

            @pl.when(target == me)
            def _():
                own[...] = value

        return carry

    lax.fori_loop(0, owners // each, batch, 0)
    value = own[...]
    for step in range(1, owners):
        source = lax.rem(me + step, owners)
        transfer(source, source).wait_recv()
        value = value + landed[source].astype(jnp.float32)
    mine[...] = value
    across = []
    for step in range(1, groups):
        peer = lax.rem(group + step, groups)
        across.append(
            pltpu.make_async_remote_copy(
                src_ref=mine,
                dst_ref=others.at[step],
                send_sem=send_group.at[step],
                recv_sem=recv_group.at[step],
                device_id={"freq": peer},
                device_id_type=MESH,
            )
        )
        across[-1].start()
    out_ref[pl.ds(pl.multiple_of(group * freqs, freqs), freqs), :] = value
    for step in range(1, owners):
        target = lax.rem(me + step, owners)
        transfer(target, target).wait_send()
    for step in range(1, groups):
        across[step - 1].wait_recv()
        source = lax.rem(group + groups - step, groups)
        out_ref[pl.ds(pl.multiple_of(source * freqs, freqs), freqs), :] = others[step]
    for copy in across:
        copy.wait_send()


def ground_sums(spectrum, absorption, count, layer, length, weight, ground, owners, groups):
    freqs = absorption.shape[0]
    rows = count.shape[1]
    chunk = 1024
    low_size = GROUND // owners
    rays = rows // spectrum.shape[1]
    each = min(4, owners)
    return pl.pallas_call(
        functools.partial(ground_kernel, chunk, rays, owners, groups, each),
        out_shape=jax.ShapeDtypeStruct((groups * freqs, low_size), jnp.float32),
        in_specs=[pl.BlockSpec(memory_space=VMEM)] * 7,
        out_specs=pl.BlockSpec(memory_space=VMEM),
        scratch_shapes=[
            pltpu.VMEM((spectrum.shape[1], chunk), jnp.bfloat16),
            pltpu.VMEM((freqs, rows), jnp.bfloat16),
            pltpu.VMEM((low_size, rows), jnp.bfloat16),
            pltpu.VMEM((each * freqs, chunk), jnp.bfloat16),
            pltpu.VMEM((each * freqs, low_size), jnp.float32),
            pltpu.VMEM((freqs, low_size), jnp.float32),
            pltpu.VMEM((owners, freqs, low_size), jnp.bfloat16),
            pltpu.VMEM((owners, freqs, low_size), jnp.bfloat16),
            pltpu.VMEM((freqs, low_size), jnp.float32),
            pltpu.VMEM((groups, freqs, low_size), jnp.float32),
            pltpu.SemaphoreType.DMA((owners,)),
            pltpu.SemaphoreType.DMA((owners,)),
            pltpu.SemaphoreType.DMA((groups,)),
            pltpu.SemaphoreType.DMA((groups,)),
        ],
        compiler_params=pltpu.CompilerParams(
            vmem_limit_bytes=48 * 1024 * 1024,
            collective_id=2,
            has_side_effects=True,
        ),
        name="ground",
    )(spectrum, absorption, count, layer, length, weight, ground)


def shards(
    sources,
    panel_pos,
    normal_angles,
    observer_angles,
    absorption,
    ray_count,
    ray_layer,
    ray_length,
    ray_weight,
    ray_ground,
):
    groups = lax.axis_size("freq")
    owners = lax.axis_size("panel")
    freqs = absorption.shape[0] // groups
    freq_start = lax.axis_index("freq") * freqs
    table = jnp.asarray(dft_rows(SAMPLES, BIN0, groups, freqs)).astype(jnp.bfloat16)
    partial_value = lax.dot_general(
        table,
        sources.reshape(-1, SAMPLES),
        (((1,), (1,)), ((), ())),
        preferred_element_type=jnp.float32,
    )
    partial_value = partial_value.reshape(2 * groups * freqs, 2, sources.shape[1])
    spectra = lax.all_to_all(partial_value, "freq", split_axis=0, concat_axis=2, tiled=True)
    spectra = spectra.transpose(1, 0, 2).reshape(4 * freqs, -1)
    weighting = GAIN / math.sqrt(panel_pos.shape[1] * owners)
    spectrum = radiate(
        spectra, panel_pos, normal_angles, observer_angles, owners, groups, weighting
    )
    obs_spectrum = (
        spectrum.reshape(2, freqs, -1).transpose(2, 1, 0).reshape(-1, 2 * freqs)
    )
    own_absorption = lax.dynamic_slice_in_dim(absorption, freq_start, freqs, 0)
    ground_power = ground_sums(
        spectrum,
        own_absorption,
        ray_count.reshape(1, -1),
        ray_layer,
        ray_length,
        ray_weight.reshape(1, -1),
        ray_ground.reshape(1, -1),
        owners,
        groups,
    )
    return (obs_spectrum, ground_power)


def solution(mesh):
    return jax.shard_map(
        shards,
        mesh=mesh,
        in_specs=(
            P(None, ("panel", "freq"), None),
            P(None, "panel"),
            P(None, "panel"),
            P(),
            P(),
            P("panel"),
            P(None, "panel"),
            P(None, "panel"),
            P("panel"),
            P("panel"),
        ),
        out_specs=(P("panel", "freq"), P(None, "panel")),
        check_vma=False,
    )
```

profile of v0, /device:TPU:0, one launch (start us, length us, event | category | flops | bytes accessed | tf_op | source)
XLA Modules:
  0.0 58.9 jit_solution(2876388747099155524)
XLA Ops:
  0.6 0.0 copy-start
  0.6 1.0 %copy-done = bf16[2,128,1024]{2,1,0:T(8,128)(2,1)S(1)} copy-done((bf16[2,128,1024]{2,1,0:T(8,128)(2,1)S(1)}, bf16[2,128,1024]{2,1,0:T(8,128)(2,1)}, u32[]{:S(2)}) %copy-start) | copy-done | bytes 524312
  1.7 1.3 %fusion = f32[128,2,128]{2,0,1:T(8,128)S(1)} fusion(bf16[128,1024,1]{1,0,2:T(8,128)(2,1)} %constant.17, bf16[2,128,1024]{2,1,0:T(8,128)(2,1)S(1)} %copy-done), kind=kOutput, calls=%fused_computation.1 | convolution fusion | flops 67108864 | bytes 917504 | tf_op jit(solution)/shard_map/dot_general | solution.py:634
  2.9 0.0 copy-start.2
  3.0 0.0 copy-start.3
  3.0 0.0 copy-start.4
  3.0 0.0 copy-start.5
  3.0 0.0 copy-start.6
  3.0 0.8 %copy.17 = f32[128,2,128]{2,1,0:T(2,128)} copy(f32[128,2,128]{2,0,1:T(8,128)S(1)} %fusion) | data formatting | bytes 262144 | tf_op jit(solution)/shard_map/dot_general | solution.py:634
  3.8 4.3 %all-to-all-start = ((f32[128,2,128]{2,1,0:T(2,128)}), f32[128,2,128]{2,1,0:T(2,128)S(1)}, u32[]{:S(2)}, u32[]{:S(2)}) async-start(f32[128,2,128]{2,1,0:T(2,128)} %copy.17), calls=%async_computation | async-start | bytes 262144 | tf_op jit(solution)/shard_map/all_to_all | solution.py:641
  8.0 0.8 %constant_dynamic-slice_fusion = f32[32,16]{0,1:T(8,128)S(1)} fusion(f32[64,16]{0,1:T(8,128)} %param.16, s32[]{:T(128)S(6)} %select_n.3), kind=kLoop, calls=%fused_computation | loop fusion | bytes 4100 | tf_op jit(solution)/shard_map/dynamic_slice | solution.py:650
  8.8 0.1 copy.21.absorption_ref
  8.9 3.7 %all-to-all-done = f32[128,2,128]{2,1,0:T(2,128)S(1)} async-done(((f32[128,2,128]{2,1,0:T(2,128)}), f32[128,2,128]{2,1,0:T(2,128)S(1)}, u32[]{:S(2)}, u32[]{:S(2)}) %all-to-all-start) | async-done | bytes 131104 | tf_op jit(solution)/shard_map/all_to_all | solution.py:641
  12.6 0.1 copy.18
  12.7 0.8 %all_to_all.16 = f32[64,2,256]{2,0,1:T(8,128)} reshape(f32[64,2,2,128]{3,2,0,1:T(2,128)S(1)} %copy.18) | data formatting | bytes 262144 | tf_op jit(solution)/shard_map/all_to_all | solution.py:641
  13.4 20.6 %radiate.1.spectrum_ref = f32[64,128]{1,0:T(8,128)} custom-call(f32[128,256]{1,0:T(8,128)} %bitcast.23, f32[3,256]{1,0:T(4,128)} %pos_ref.1, f32[2,256]{1,0:T(2,128)} %normal_ref.1, f32[2,2048]{1,0:T(2,128)} %angle_ref.1, f32[2,2,32,3072]{3,2,1,0:T(8,128)} %constant.15.clone.table_ref), custom_call_target="tpu_custom_call" | custom-call | tf_op jit(solution)/shard_map/radiate/pallas_call | solution.py:419
  34.0 1.4 %copy.19 = f32[128,32,2]{0,2,1:T(2,128)} copy(f32[128,32,2]{0,1,2:T(8,128)} %bitcast.18) | data formatting | bytes 65536 | tf_op jit(solution)/shard_map/transpose | solution.py:648
  35.4 0.0 copy-done.2
  35.4 0.0 copy-done.3
  35.4 0.0 copy-done.4
  35.4 0.0 copy-done.5
  35.4 0.0 copy-done.6
  35.4 0.0 copy-start.1
  35.4 0.7 %copy-done.1 = f32[64,128]{1,0:T(8,128)S(1)} copy-done((f32[64,128]{1,0:T(8,128)S(1)}, f32[64,128]{1,0:T(8,128)}, u32[]{:S(2)}) %copy-start.1) | copy-done | bytes 32792
  36.2 22.1 %ground.1 = f32[64,256]{1,0:T(8,128)S(1)} custom-call(f32[64,128]{1,0:T(8,128)S(1)} %copy-done.1, f32[32,16]{1,0:T(8,128)S(1)} %copy.21.absorption_ref, s32[1,8192]{1,0:T(1,128)S(1)} %bitcast.19, s32[8,8192]{1,0:T(8,128)S(1)} %copy-done.2, f32[8,8192]{1,0:T(8,128)S(1)} %copy-done.3, f32[1,8192]{1,0:T(1,128)S(1)} %bitcast.20, s32[1,8192]{1,0:T(1,128)S(1)} %bitcast.21), custom_call_target="tpu_custom_call" | custom-call | tf_op jit(solution)/shard_map/ground/pallas_call | solution.py:587
  58.3 0.6 %copy.23 = f32[64,256]{1,0:T(8,128)} copy(f32[64,256]{1,0:T(8,128)S(1)} %ground.1) | data formatting | bytes 131072
Async XLA Ops:
  0.6 1.0 %copy-start = (bf16[2,128,1024]{2,1,0:T(8,128)(2,1)S(1)}, bf16[2,128,1024]{2,1,0:T(8,128)(2,1)}, u32[]{:S(2)}) copy-start(bf16[2,128,1024]{2,1,0:T(8,128)(2,1)} %param.12) | copy-start | bytes 1572868
  2.9 32.5 %copy-start.2 = (s32[8,8192]{1,0:T(8,128)S(1)}, s32[8,8192]{1,0:T(8,128)}, u32[]{:S(2)}) copy-start(s32[8,8192]{1,0:T(8,128)} %layer_ref.1) | copy-start | bytes 786436
  3.0 32.5 %copy-start.3 = (f32[8,8192]{1,0:T(8,128)S(1)}, f32[8,8192]{1,0:T(8,128)}, u32[]{:S(2)}) copy-start(f32[8,8192]{1,0:T(8,128)} %length_ref.1) | copy-start | bytes 786436
  3.0 32.4 %copy-start.4 = (s32[8192]{0:T(1024)S(1)}, s32[8192]{0:T(1024)}, u32[]{:S(2)}) copy-start(s32[8192]{0:T(1024)} %param.17) | copy-start | bytes 98308
  3.0 32.4 %copy-start.5 = (f32[8192]{0:T(1024)S(1)}, f32[8192]{0:T(1024)}, u32[]{:S(2)}) copy-start(f32[8192]{0:T(1024)} %param.20) | copy-start | bytes 98308
  3.0 32.4 %copy-start.6 = (s32[8192]{0:T(1024)S(1)}, s32[8192]{0:T(1024)}, u32[]{:S(2)}) copy-start(s32[8192]{0:T(1024)} %param.21) | copy-start | bytes 98308
  3.8 8.8 %all-to-all-start = ((f32[128,2,128]{2,1,0:T(2,128)}), f32[128,2,128]{2,1,0:T(2,128)S(1)}, u32[]{:S(2)}, u32[]{:S(2)}) async-start(f32[128,2,128]{2,1,0:T(2,128)} %copy.17), calls=%async_computation | async-start | bytes 262144 | tf_op jit(solution)/shard_map/all_to_all | solution.py:641
  35.4 0.8 %copy-start.1 = (f32[64,128]{1,0:T(8,128)S(1)}, f32[64,128]{1,0:T(8,128)}, u32[]{:S(2)}) copy-start(f32[64,128]{1,0:T(8,128)} %radiate.1.spectrum_ref) | copy-start | bytes 98308
where the time goes:
time: 59.4 us; the launch traced here: 58.9 us
  Pallas kernels  42.7 us (72%)
  local copies, waits for them, and re-layouts  6.31 us (11%)
  starting transfers between devices  4.26 us (7%)
  waiting for transfers between devices  3.71 us (6%)
  matrix products  1.26 us (2%)
  between operations  0.74 us (1%)
    pallas_call x1, Pallas kernels, ground_sums(): pl.pallas_call(functools.partial(ground_kernel, chunk, rays, owners, grou...  22.1 us
    pallas_call x1, Pallas kernels, radiate(): pl.pallas_call(functools.partial(radiate_kernel, freqs, panels, lanes), o...  20.6 us
    all_to_all x1, starting transfers between devices, shards(): lax.all_to_all(partial_value, 'freq', split_axis=0, concat_axis=2, tiled=...  4.26 us
    all_to_all x1, waiting for transfers between devices, shards(): lax.all_to_all(partial_value, 'freq', split_axis=0, concat_axis=2, tiled=...  3.71 us
    unnamed x16, local copies, waits for them, and re-layouts  2.53 us
    transpose x1, local copies, waits for them, and re-layouts, shards(): spectrum.reshape(2, freqs, -1).transpose(2, 1, 0).reshape(-1, 2 * freqs)  1.4 us
    dot_general x1, matrix products, shards(): lax.dot_general(table, sources.reshape(-1, SAMPLES), (((1,), (1,)), ((),...  1.26 us
  transfers between devices with their start and end apart: 1, of which 1 were waited for; matrix products, arithmetic and copies ran while one was open for 1% of the time, Pallas kernels for 0%

commit v1 on v0

v1 whole, which is shorter than its diff:
```python
import functools
import math

import jax
import jax.numpy as jnp
import numpy as np
from jax import lax
from jax.experimental import pallas as pl
from jax.experimental.pallas import tpu as pltpu
from jax.sharding import PartitionSpec as P

SAMPLES = 1024
BIN0 = 32
RADIUS = 150.0
GAIN = 3.0
GROUND = 4096
REACH = 52.0
BLOCK = 16
BLOCKS = 3
ORDERS = BLOCK * BLOCKS
UNITS = BLOCK * BLOCKS * (BLOCKS + 1) // 2
TOP = 56
MESH = pl.DeviceIdType.MESH
VMEM = pltpu.MemorySpace.VMEM


def dft_rows(samples, first_bin, groups, per_group):
    index = np.arange(samples)
    bins = first_bin + np.arange(groups * per_group)
    angle = 2.0 * np.pi / samples * (bins[:, None] * index[None, :] % samples)
    window = (0.5 - 0.5 * np.cos(2.0 * np.pi / samples * index)) / math.sqrt(samples)
    rows = np.stack([window * np.cos(angle), -window * np.sin(angle)])
    rows = rows.reshape(2, groups, per_group, samples).transpose(1, 0, 2, 3)
    return rows.reshape(-1, samples).astype(np.float32)


def sincos_turns(turns):
    part = turns - jnp.round(turns)
    square = part * part
    sine = jnp.float32(-(math.pi**11) / math.factorial(11))
    for power in (9, 7, 5, 3, 1):
        sign = 1.0 if power % 4 == 1 else -1.0
        sine = sine * square + sign * math.pi**power / math.factorial(power)
    sine = sine * part
    cosine = jnp.float32(math.pi**12 / math.factorial(12))
    for power in (10, 8, 6, 4, 2, 0):
        sign = 1.0 if power % 4 == 0 else -1.0
        cosine = cosine * square + sign * math.pi**power / math.factorial(power)
    return 1.0 - 2.0 * sine * sine, 2.0 * sine * cosine


def enter(axis, count):
    barrier = pltpu.get_barrier_semaphore()
    me = lax.axis_index(axis)
    for step in range(1, count):
        pl.semaphore_signal(
            barrier, inc=1, device_id={axis: lax.rem(me + step, count)}, device_id_type=MESH
        )
    return barrier


def split_float(value):
    pieces = []
    for _ in range(2):
        pieces.append(value.astype(jnp.bfloat16))
        value = value - pieces[-1].astype(jnp.float32)
    return pieces


def unit_base(block):
    return sum(ORDERS - BLOCK * earlier for earlier in range(block))


def expansion_table(groups, freqs, weighting):
    wave = 2.0 * np.pi / SAMPLES * (BIN0 + np.arange(groups * freqs))
    reach = wave * RADIUS
    below = np.exp(-1j * reach) / reach * 1j
    hankel = [below, (1 / reach + 1j) * below]
    for n in range(1, ORDERS):
        hankel.append((2 * n + 1) / reach * hankel[n] - hankel[n - 1])
    hankel = np.stack(hankel[:ORDERS])
    radial = (RADIUS * weighting) * (-1j * wave)[None] * hankel
    rows = np.zeros((2, groups * freqs, UNITS * 2 * BLOCK))
    start = 2.0
    for m in range(ORDERS):
        if m:
            start *= 4 * m * m / (2 * m * (2 * m + 1))
        norm = start * (np.pi if m else 2 * np.pi)
        block = m // BLOCK
        for n in range(m, ORDERS):
            if n > m:
                norm *= 4 * (n * n - m * m) / (4 * n * n - 1)
            at = (unit_base(block) + n - BLOCK * block) * 2 * BLOCK + m - BLOCK * block
            value = 4 * np.pi / norm * radial[n]
            for side in range(2 if m else 1):
                rows[0, :, at + BLOCK * side] = value.real
                rows[1, :, at + BLOCK * side] = value.imag
    rows = rows.reshape(2, groups, freqs, -1).transpose(1, 0, 2, 3)
    return rows.astype(np.float32)


def times(left, right):
    return (left[0] * right[0] - left[1] * right[1], left[0] * right[1] + left[1] * right[0])


def azimuth_powers(real, imaginary, shape):
    one = (jnp.broadcast_to(real, shape), jnp.broadcast_to(imaginary, shape))
    row = lax.broadcasted_iota(jnp.int32, shape, 0)
    square = times(one, one)
    fourth = times(square, square)
    eighth = times(fourth, fourth)
    first = None
    for bit, power in ((1, one), (2, square), (4, fourth)):
        picked = (jnp.where(row & bit, power[0], 1.0), jnp.where(row & bit, power[1], 0.0))
        first = picked if first is None else times(first, picked)
    tiles = [first]
    for _ in range(ORDERS // 8 - 1):
        tiles.append(times(tiles[-1], eighth))
    seventh = times(times(fourth, square), one)
    before = [(pltpu.roll(first[0], 1, axis=0), pltpu.roll(first[1], 1, axis=0))]
    before += [times(tile, seventh) for tile in tiles[:-1]]
    return tiles, before


def join(tiles, block, part):
    per = BLOCK // 8
    return jnp.concatenate([tile[part] for tile in tiles[block * per : (block + 1) * per]], axis=0)


def kernel(freqs, panels, lanes, sources_hbm, dft_hbm, pos_hbm, normal_hbm, angle_hbm, table_hbm,
           absorption_hbm, count_hbm, layer_hbm, length_hbm, weight_hbm, ground_hbm, spectrum_ref,
           power_ref, sources, dft, pos_ref, normal_ref, angle_ref, table, absorption_ref, count_ref,
           layer_ref, length_ref, weight_ref, ground_ref, outgoing, incoming, directions, basis,
           moments, radial, sums, mine, theirs, weights, parts, landed, upright, damped, spreading,
           energies, lows, left, total, own, pieces, arrived, final, others, fetch_sem, cross_send,
           cross_recv, pair_send, pair_recv, send_sem, recv_sem, piece_send, piece_recv, last_send,
           last_recv):
    owners = 2 * parts.shape[0]
    half = owners // 2
    me = lax.axis_index("panel")
    core = lax.rem(me, 2)
    chip = lax.div(me, 2)
    sibling = me + 1 - 2 * core
    group = lax.axis_index("freq")
    groups = outgoing.shape[0]
    each_part = sources.shape[1]
    step = 2.0 * math.pi / SAMPLES
    pairs = [
        (angle_hbm, angle_ref),
        (sources_hbm, sources),
        (dft_hbm, dft),
        (pos_hbm, pos_ref),
        (normal_hbm, normal_ref),
        (table_hbm.at[group], table),
        (layer_hbm, layer_ref),
        (length_hbm, length_ref),
        (count_hbm, count_ref),
        (weight_hbm, weight_ref),
        (ground_hbm, ground_ref),
        (absorption_hbm, absorption_ref),
    ]
    fetches = [
        pltpu.make_async_copy(pair[0], pair[1], fetch_sem.at[n]) for n, pair in enumerate(pairs)
    ]
    for fetch in fetches:
        fetch.start()
    barrier = enter("panel", owners)
    enter("freq", groups)

    def pair_copy(chunk):
        at = pl.ds(pl.multiple_of(chunk * 128, 128), 128)
        return pltpu.make_async_remote_copy(
            src_ref=mine.at[:, at],
            dst_ref=theirs.at[:, at],
            send_sem=pair_send.at[chunk],
            recv_sem=pair_recv.at[chunk],
            device_id={"panel": sibling},
            device_id_type=MESH,
        )

    def transfer(source, target):
        return pltpu.make_async_remote_copy(
            src_ref=parts.at[target],
            dst_ref=landed.at[source],
            send_sem=send_sem.at[target],
            recv_sem=recv_sem.at[source],
            device_id={"panel": 2 * target + core},
            device_id_type=MESH,
        )

    def cross(source, target):
        return pltpu.make_async_remote_copy(
            src_ref=outgoing.at[target],
            dst_ref=incoming.at[source],
            send_sem=cross_send.at[target],
            recv_sem=cross_recv.at[source],
            device_id={"freq": target},
            device_id_type=MESH,
        )

    fetches[0].wait()
    for order in range(half):
        both = angle_ref[:, 2 * order * lanes : 2 * (order + 1) * lanes]
        angle = jnp.where(core == 0, both[:, 0:lanes], both[:, lanes : 2 * lanes])
        cosine, sine = sincos_turns(angle * jnp.float32(0.5 / math.pi))
        to = slice(order * lanes, (order + 1) * lanes)
        directions[0:1, to] = sine[0:1] * cosine[1:2]
        directions[1:2, to] = sine[0:1] * sine[1:2]
        directions[2:3, to] = -cosine[0:1]
    fetches[1].wait()
    fetches[2].wait()
    lines = jnp.concatenate([sources[0], sources[1]], axis=0)
    bins_of = lax.dot_general(
        dft[...], lines, (((1,), (1,)), ((), ())), preferred_element_type=jnp.float32
    )
    for n in range(groups):
        outgoing[n] = bins_of[n * 2 * freqs : (n + 1) * 2 * freqs]
    pl.semaphore_wait(barrier, owners + groups - 2)
    for n in range(1, groups):
        peer = lax.rem(group + n, groups)
        cross(group, peer).start()
    incoming[group] = outgoing[group]
    row = lax.broadcasted_iota(jnp.int32, (BLOCK, 128), 0)

    def spread_out(value, width):
        return jnp.concatenate([value] * (width // 128), axis=1)

    def slope(order, block, width):
        m = (row + BLOCK * block).astype(jnp.float32)
        value = (float(order * order) - m * m) * (4.0 / (4.0 * order * order - 1.0))
        return spread_out(value, width)

    wide = 512

    def observe(index, carry):
        at = pl.ds(pl.multiple_of(index * wide, wide), wide)
        shape = (BLOCK, wide)
        rows = spread_out(row, wide)
        tiles = azimuth_powers(directions[0:1, at], directions[1:2, at], (8, wide))[0]
        double = jnp.broadcast_to(2.0 * directions[2:3, at], shape)
        for block in range(BLOCKS):
            first = BLOCK * block
            cosines, sines = join(tiles, block, 0), join(tiles, block, 1)
            now = jnp.where(rows == 0, 1.0, 0.0)
            past = jnp.zeros(shape, jnp.float32)
            for order in range(first, ORDERS):
                begin = (unit_base(block) + order - first) * 2 * BLOCK
                basis[begin : begin + BLOCK, at] = (now * cosines).astype(jnp.bfloat16)
                basis[begin + BLOCK : begin + 2 * BLOCK, at] = (now * sines).astype(jnp.bfloat16)
                if order + 1 < ORDERS:
                    later = double * now - slope(order, block, wide) * past
                    if order + 1 - first < BLOCK:
                        later = jnp.where(rows == order + 1 - first, 1.0, later)
                    past, now = now, later
        return carry

    lax.fori_loop(0, half * lanes // wide, observe, 0)

    def emit(unit, part, at, value):
        high = value.astype(jnp.bfloat16)
        low = (value - high.astype(jnp.float32)).astype(jnp.bfloat16)
        moments[unit, part * BLOCK : (part + 1) * BLOCK, at] = high
        moments[unit, (2 + part) * BLOCK : (3 + part) * BLOCK, at] = low

    broad = 256 if panels % 256 == 0 else 128

    def locate(index, carry):
        at = pl.ds(pl.multiple_of(index * broad, broad), broad)
        beside = pl.ds(pl.multiple_of(panels + index * broad, broad), broad)
        shape = (BLOCK, broad)
        rows = spread_out(row, broad)
        place = pos_ref[:, at] * jnp.float32(1.0 / REACH)
        cosine, sine = sincos_turns(normal_ref[:, at] * jnp.float32(0.5 / math.pi))
        normal = [sine[0:1] * cosine[1:2], sine[0:1] * sine[1:2], cosine[0:1]]
        across = sum(place[n : n + 1] * normal[n] for n in range(3))
        square = sum(place[n : n + 1] * place[n : n + 1] for n in range(3))
        tiles, before = azimuth_powers(place[0:1], place[1:2], (8, broad))
        tilt = (
            jnp.broadcast_to(normal[0], (8, broad)),
            jnp.broadcast_to(normal[1], (8, broad)),
        )
        turned = [times(value, tilt) for value in before]
        double = jnp.broadcast_to(2.0 * place[2:3], shape)
        lean = jnp.broadcast_to(2.0 * normal[2], shape)
        size = jnp.broadcast_to(square, shape)
        grow = jnp.broadcast_to(2.0 * across, shape)
        for block in range(BLOCKS):
            first = BLOCK * block
            cosines, sines = join(tiles, block, 0), join(tiles, block, 1)
            m = (rows + first).astype(jnp.float32)
            cosines_by = join(turned, block, 0) * m
            sines_by = join(turned, block, 1) * m
            now = jnp.where(rows == 0, 1.0, 0.0)
            past = rate = rate_past = jnp.zeros(shape, jnp.float32)
            for order in range(first, ORDERS):
                unit = unit_base(block) + order - first
                emit(unit, 0, at, now * cosines)
                emit(unit, 1, at, now * sines)
                emit(unit, 0, beside, rate * cosines + now * cosines_by)
                emit(unit, 1, beside, rate * sines + now * sines_by)
                if order + 1 < ORDERS:
                    beta = slope(order, block, broad)
                    beta_size = beta * size
                    later = double * now - beta_size * past
                    rate_later = (lean * now + double * rate) - (
                        (beta * grow) * past + beta_size * rate_past
                    )
                    if order + 1 - first < BLOCK:
                        later = jnp.where(rows == order + 1 - first, 1.0, later)
                    past, now = now, later
                    rate_past, rate = rate, rate_later
        return carry

    fetches[3].wait()
    fetches[4].wait()
    lax.fori_loop(0, panels // broad, locate, 0)
    place = pos_ref[...]
    cosine, sine = sincos_turns(normal_ref[...] * jnp.float32(0.5 / math.pi))
    across = (
        sine[0:1] * cosine[1:2] * place[0:1]
        + sine[0:1] * sine[1:2] * place[1:2]
        + cosine[0:1] * place[2:3]
    )
    square = place[0:1] * place[0:1] + place[1:2] * place[1:2] + place[2:3] * place[2:3]
    length = square * lax.rsqrt(jnp.maximum(square, 1e-30))
    bins = lax.broadcasted_iota(jnp.int32, (freqs, panels), 0) + (BIN0 + group * freqs)
    wave = bins.astype(jnp.float32) * jnp.float32(step)
    size = square * jnp.float32(1.0 / REACH**2)
    argument = wave * length
    log_start = (
        12.0 * math.log(10.0)
        - math.lgamma(2 * TOP + 3)
        + (TOP + 1) * math.log(2.0)
        + math.lgamma(TOP + 2)
    )
    kappa = wave * jnp.float32(REACH)
    inverse = 1.0 / kappa
    later = jnp.zeros((freqs, panels), jnp.float32)
    now = jnp.exp(
        TOP * jnp.log(kappa) + jnp.float32(log_start) - argument * argument / (4.0 * TOP + 6.0)
    )
    size = jnp.broadcast_to(size, (freqs, panels))
    for order in range(TOP, 0, -1):
        earlier = (float(2 * order + 1) * inverse) * now - size * later
        later, now = now, earlier
        if order - 1 <= ORDERS:
            radial[order - 1] = now
    near = later * (length * jnp.float32(1.0 / REACH))
    cosine, sine = sincos_turns(argument * jnp.float32(0.5 / math.pi))
    safe = jnp.maximum(argument, 0.05)
    over = 1.0 / safe
    small = argument < 0.05
    zero = jnp.where(small, 1.0 - argument * argument * (1.0 / 6.0), sine * over)
    one = jnp.where(small, argument * (1.0 / 3.0), (sine * over - cosine) * over)
    scale = (now * zero + near * one) / (now * now + near * near)
    heavy = scale * wave

    def both(value):
        return jnp.concatenate([value, value], axis=0)

    for n in range(1, groups):
        source = lax.rem(group + n, groups)
        cross(source, source).wait_recv()
    spectra = [
        jnp.concatenate(
            [incoming[n, :, side * each_part : (side + 1) * each_part] for n in range(groups)],
            axis=1,
        )
        for side in range(2)
    ]
    monopole = jnp.concatenate(
        [-heavy * spectra[0][freqs : 2 * freqs], heavy * spectra[0][0:freqs]], axis=0
    )
    loading = spectra[1] * both(scale)
    facing = loading * both(-wave * across * jnp.float32(1.0 / REACH))
    loading = loading * jnp.float32(1.0 / REACH)
    sums[0] = monopole
    sums[1] = facing
    sums[2] = loading

    def project(blocks, quad, carry):
        values = [[] for _ in range(blocks)]
        for inner in range(4):
            order = quad * 4 + inner
            here, above = both(radial[order]), both(radial[order + 1])
            strength = jnp.concatenate(
                [sums[0] * here + sums[1] * above, sums[2] * here], axis=1
            )
            high = strength.astype(jnp.bfloat16).astype(jnp.float32)
            right = jnp.concatenate([high, strength - high], axis=0).astype(jnp.bfloat16)
            left = jnp.concatenate(
                [moments[unit_base(b) - BLOCK * b + order] for b in range(blocks)], axis=0
            )
            product = lax.dot_general(
                left, right, (((1,), (1,)), ((), ())), preferred_element_type=jnp.float32
            )
            for b in range(blocks):
                begin = 4 * BLOCK * b
                values[b].append(
                    product[begin : begin + 2 * BLOCK]
                    + product[begin + 2 * BLOCK : begin + 4 * BLOCK]
                )
        for b in range(blocks):
            turned = jnp.transpose(jnp.concatenate(values[b], axis=0))
            chunk = (unit_base(b) - BLOCK * b) // 4 + quad
            at = pl.ds(pl.multiple_of(chunk * 128, 128), 128)
            mine[:, at] = turned[0 : 2 * freqs] + turned[2 * freqs : 4 * freqs]
            pair_copy(chunk).start()
        return carry

    per = BLOCK // 4
    for section in range(BLOCKS):
        lax.fori_loop(
            section * per, (section + 1) * per, functools.partial(project, section + 1), 0
        )
    fetches[5].wait()

    def merge(chunk, carry):
        pair_copy(chunk).wait_recv()
        at = pl.ds(pl.multiple_of(chunk * 128, 128), 128)
        value = mine[:, at] + theirs[:, at]
        real, imaginary = value[0:freqs], value[freqs : 2 * freqs]
        by_real, by_imaginary = table[0, :, at], table[1, :, at]
        value = jnp.concatenate(
            [
                real * by_real - imaginary * by_imaginary,
                real * by_imaginary + imaginary * by_real,
            ],
            axis=0,
        )
        high = value.astype(jnp.bfloat16).astype(jnp.float32)
        weights[:, at] = jnp.concatenate([high, value - high], axis=0).astype(jnp.bfloat16)
        return carry

    lax.fori_loop(0, UNITS // 4, merge, 0)
    each = 2 if half % 2 == 0 else 1

    def field(order, carry):
        pick = lax.rem(lax.div(chip, each) + 1 + order, half // each)
        at = pl.ds(pl.multiple_of(pick * (each * lanes), each * lanes), each * lanes)
        product = jnp.dot(weights[...], basis[:, at], preferred_element_type=jnp.float32)
        product = product[0 : 2 * freqs] + product[2 * freqs : 4 * freqs]
        for side in range(each):
            target = pick * each + side
            parts[target] = product[:, side * lanes : (side + 1) * lanes]

            @pl.when(target != chip)
            def _():
                transfer(chip, target).start()

        return carry

    lax.fori_loop(0, half // each, field, 0)
    for fetch in fetches[6:]:
        fetch.wait()
    observers = lanes
    rays_all = count_ref.shape[1]
    rays = rays_all // observers
    chunk = left.shape[1]
    chunks = rays_all // chunk
    each_batch = left.shape[0] // freqs
    layers = absorption_ref.shape[0]
    low_size = power_ref.shape[1]
    upright[...] = jnp.transpose(absorption_ref[...])
    split = split_float(upright[pl.ds(pl.multiple_of(group * freqs, freqs), freqs), :])
    absorb = jnp.concatenate([split[i] for i in (0, 0, 1)], axis=1)
    wide_shape = (observers, chunk)
    begin = lax.broadcasted_iota(jnp.int32, wide_shape, 0) * rays
    column = lax.broadcasted_iota(jnp.int32, wide_shape, 1)
    same_owner = (column >= begin) & (column < begin + rays)
    spreading[...] = jnp.where(same_owner, 1.0, 0.0).astype(jnp.bfloat16)

    def piece_copy(source, target):
        return pltpu.make_async_remote_copy(
            src_ref=pieces.at[target],
            dst_ref=arrived.at[source],
            send_sem=piece_send.at[target],
            recv_sem=piece_recv.at[source],
            device_id={"panel": target},
            device_id_type=MESH,
        )

    def prepare(index, carry):
        at = pl.ds(pl.multiple_of(index * chunk, chunk), chunk)
        layer_ids = lax.broadcasted_iota(jnp.int32, (layers, chunk), 0)
        count = count_ref[0:1, at]
        lengths = jnp.zeros((layers, chunk), jnp.float32)
        for segment in range(layer_ref.shape[0]):
            used = jnp.where(segment < count, length_ref[segment : segment + 1, at], 0.0)
            same = layer_ref[segment : segment + 1, at] == layer_ids
            lengths = lengths + jnp.where(same, used, 0.0)
        split = split_float(lengths)
        lengths = jnp.concatenate([split[i] for i in (0, 1, 0)], axis=0)
        depth = jnp.dot(absorb, lengths, preferred_element_type=jnp.float32)
        damped[:, at] = weight_ref[0:1, at] * jnp.exp(-depth)
        within = ground_ref[0:1, at] & (low_size - 1)
        ids = lax.broadcasted_iota(jnp.int32, (low_size, chunk), 0)
        lows[:, at] = jnp.where(ids == within, 1.0, 0.0).astype(jnp.bfloat16)
        return carry

    lax.fori_loop(0, chunks, prepare, 0)
    value = parts[chip]
    for n in range(1, half):
        source = lax.rem(chip + n, half)
        transfer(source, source).wait_recv()
        value = value + landed[source]
    real, imaginary = value[0:freqs], value[freqs : 2 * freqs]
    spectrum_ref[pl.ds(0, freqs, 2), :] = real
    spectrum_ref[pl.ds(1, freqs, 2), :] = imaginary
    power = real * real + imaginary * imaginary

    def spread(index, carry):
        at = pl.ds(pl.multiple_of(index * chunk, chunk), chunk)
        turned = pltpu.roll(power, lax.rem(observers - index * (chunk // rays), observers), axis=1)
        value = jnp.dot(
            jnp.concatenate(split_float(turned), axis=0),
            spreading[...],
            preferred_element_type=jnp.float32,
        )
        value = value[0:freqs] + value[freqs : 2 * freqs]
        energies[:, at] = (value * damped[:, at]).astype(jnp.bfloat16)
        return carry

    lax.fori_loop(0, chunks, spread, 0)

    def batch(order, carry):
        base = lax.rem(lax.div(me, each_batch) + 1 + order, owners // each_batch) * each_batch
        total[...] = jnp.zeros_like(total)

        def accumulate(index, carry):
            at = pl.ds(pl.multiple_of(index * chunk, chunk), chunk)
            block = ground_ref[0:1, at] // low_size
            for n in range(each_batch):
                keep = jnp.where(block == base + n, 1.0, 0.0).astype(jnp.bfloat16)
                left[n * freqs : (n + 1) * freqs, :] = energies[:, at] * keep
            total[...] += lax.dot_general(
                left[...],
                lows[:, at],
                (((1,), (1,)), ((), ())),
                preferred_element_type=jnp.float32,
            )
            return carry

        lax.fori_loop(0, chunks, accumulate, 0)
        for n in range(each_batch):
            target = base + n
            value = total[n * freqs : (n + 1) * freqs, :]
            pieces[target] = value.astype(jnp.bfloat16)

            @pl.when(target != me)
            def _():
                piece_copy(me, target).start()

            @pl.when(target == me)
            def _():
                own[...] = value

        return carry

    lax.fori_loop(0, owners // each_batch, batch, 0)
    value = own[...]
    for n in range(1, owners):
        source = lax.rem(me + n, owners)
        piece_copy(source, source).wait_recv()
        value = value + arrived[source].astype(jnp.float32)
    final[...] = value
    across_copies = []
    for n in range(1, groups):
        across_copies.append(
            pltpu.make_async_remote_copy(
                src_ref=final,
                dst_ref=others.at[n],
                send_sem=last_send.at[n],
                recv_sem=last_recv.at[n],
                device_id={"freq": lax.rem(group + n, groups)},
                device_id_type=MESH,
            )
        )
        across_copies[-1].start()
    power_ref[pl.ds(pl.multiple_of(group * freqs, freqs), freqs), :] = value
    for n in range(1, groups):
        peer = lax.rem(group + n, groups)
        cross(peer, peer).wait_send()
    for n in range(1, half):
        target = lax.rem(chip + n, half)
        transfer(target, target).wait_send()
    for n in range(1, owners):
        target = lax.rem(me + n, owners)
        piece_copy(target, target).wait_send()

    def drain(chunk, carry):
        pair_copy(chunk).wait_send()
        return carry

    lax.fori_loop(0, UNITS // 4, drain, 0)
    for n in range(1, groups):
        across_copies[n - 1].wait_recv()
        source = lax.rem(group + groups - n, groups)
        power_ref[pl.ds(pl.multiple_of(source * freqs, freqs), freqs), :] = others[n]
    for copy in across_copies:
        copy.wait_send()


def shards(
    sources,
    panel_pos,
    normal_angles,
    observer_angles,
    absorption,
    ray_count,
    ray_layer,
    ray_length,
    ray_weight,
    ray_ground,
):
    groups = lax.axis_size("freq")
    owners = lax.axis_size("panel")
    freqs = absorption.shape[0] // groups
    panels = panel_pos.shape[1]
    observers = observer_angles.shape[1]
    lanes = observers // owners
    half = owners // 2
    depth = UNITS * 2 * BLOCK
    rows = ray_count.shape[0]
    chunk = 1024
    low_size = GROUND // owners
    each = min(8, owners)
    weighting = GAIN / math.sqrt(panels * owners)
    dft = jnp.asarray(dft_rows(SAMPLES, BIN0, groups, freqs).astype(jnp.bfloat16))
    table = jnp.asarray(expansion_table(groups, freqs, weighting))
    operands = (
        sources,
        dft,
        panel_pos,
        normal_angles,
        observer_angles,
        table,
        absorption.T,
        ray_count.reshape(1, -1),
        ray_layer,
        ray_length,
        ray_weight.reshape(1, -1),
        ray_ground.reshape(1, -1),
    )
    held = [pltpu.VMEM(value.shape, value.dtype) for value in operands]
    held[5] = pltpu.VMEM(table.shape[1:], table.dtype)
    width = 2 * sources.shape[1]
    f32, bf16 = jnp.float32, jnp.bfloat16
    spectrum, power = pl.pallas_call(
        functools.partial(kernel, freqs, panels, lanes),
        out_shape=(
            jax.ShapeDtypeStruct((2 * freqs, lanes), f32),
            jax.ShapeDtypeStruct((groups * freqs, low_size), f32),
        ),
        in_specs=[pl.BlockSpec(memory_space=pltpu.MemorySpace.HBM)] * len(operands),
        out_specs=(pl.BlockSpec(memory_space=VMEM),) * 2,
        scratch_shapes=held
        + [
            pltpu.VMEM((groups, 2 * freqs, width), f32),
            pltpu.VMEM((groups, 2 * freqs, width), f32),
            pltpu.VMEM((8, half * lanes), f32),
            pltpu.VMEM((depth, half * lanes), bf16),
            pltpu.VMEM((UNITS, 4 * BLOCK, 2 * panels), bf16),
            pltpu.VMEM((ORDERS + 1, freqs, panels), f32),
            pltpu.VMEM((3, 2 * freqs, panels), f32),
            pltpu.VMEM((2 * freqs, depth), f32),
            pltpu.VMEM((2 * freqs, depth), f32),
            pltpu.VMEM((4 * freqs, depth), bf16),
            pltpu.VMEM((half, 2 * freqs, lanes), f32),
            pltpu.VMEM((half, 2 * freqs, lanes), f32),
            pltpu.VMEM(absorption.shape, f32),
            pltpu.VMEM((freqs, rows), f32),
            pltpu.VMEM((lanes, chunk), bf16),
            pltpu.VMEM((freqs, rows), bf16),
            pltpu.VMEM((low_size, rows), bf16),
            pltpu.VMEM((each * freqs, chunk), bf16),
            pltpu.VMEM((each * freqs, low_size), f32),
            pltpu.VMEM((freqs, low_size), f32),
            pltpu.VMEM((owners, freqs, low_size), bf16),
            pltpu.VMEM((owners, freqs, low_size), bf16),
            pltpu.VMEM((freqs, low_size), f32),
            pltpu.VMEM((groups, freqs, low_size), f32),
            pltpu.SemaphoreType.DMA((len(operands),)),
            pltpu.SemaphoreType.DMA((groups,)),
            pltpu.SemaphoreType.DMA((groups,)),
            pltpu.SemaphoreType.DMA((UNITS // 4,)),
            pltpu.SemaphoreType.DMA((UNITS // 4,)),
            pltpu.SemaphoreType.DMA((half,)),
            pltpu.SemaphoreType.DMA((half,)),
            pltpu.SemaphoreType.DMA((owners,)),
            pltpu.SemaphoreType.DMA((owners,)),
            pltpu.SemaphoreType.DMA((groups,)),
            pltpu.SemaphoreType.DMA((groups,)),
        ],
        compiler_params=pltpu.CompilerParams(
            vmem_limit_bytes=65275 * 1024,
            collective_id=1,
            has_side_effects=True,
        ),
        name="spectra",
    )(*operands)
    return spectrum.T, power


def solution(mesh):
    return jax.shard_map(
        shards,
        mesh=mesh,
        in_specs=(
            P(None, ("panel", "freq"), None),
            P(None, "panel"),
            P(None, "panel"),
            P(),
            P(),
            P("panel"),
            P(None, "panel"),
            P(None, "panel"),
            P("panel"),
            P("panel"),
        ),
        out_specs=(P("panel", "freq"), P(None, "panel")),
        check_vma=False,
    )
```

time: 59.4 us -> 43.7 us (0.74)
  starting transfers between devices: 4.26 us -> 0 us
  waiting for transfers between devices: 3.71 us -> 0 us
  local copies, waits for them, and re-layouts: 6.31 us -> 2.85 us
  Pallas kernels: 42.7 us -> 40 us
  matrix products: 1.26 us -> 0 us
    all_to_all x1 -> x0, starting transfers between devices: 4.26 us -> none  [shards(): lax.all_to_all(partial_value, 'freq', split_axis=0, concat_axis=2, tiled=...]
    all_to_all x1 -> x0, waiting for transfers between devices: 3.71 us -> none  [shards(): lax.all_to_all(partial_value, 'freq', split_axis=0, concat_axis=2, tiled=...]
    pallas_call x2 -> x1, Pallas kernels: 42.7 us -> 40 us  [shards(): pl.pallas_call(functools.partial(kernel, freqs, panels, lanes), out_shape...]
    transpose x1 -> x0, local copies, waits for them, and re-layouts: 1.4 us -> none  [shards(): spectrum.reshape(2, freqs, -1).transpose(2, 1, 0).reshape(-1, 2 * freqs)]
    dot_general x1 -> x0, matrix products: 1.26 us -> none  [shards(): lax.dot_general(table, sources.reshape(-1, SAMPLES), (((1,), (1,)), ((),...]
    all_to_all x2 -> x0, local copies, waits for them, and re-layouts: 0.86 us -> none  [shards(): lax.all_to_all(partial_value, 'freq', split_axis=0, concat_axis=2, tiled=...]
    dynamic_slice x1 -> x0, local copies, waits for them, and re-layouts: 0.77 us -> none  [shards(): own_absorption = lax.dynamic_slice_in_dim(absorption, freq_start, freqs, 0)]
    dot_general x1 -> x0, local copies, waits for them, and re-layouts: 0.75 us -> none  [shards(): lax.dot_general(table, sources.reshape(-1, SAMPLES), (((1,), (1,)), ((),...]
  transfers between devices with their start and end apart: 1 -> 0, of which waited for: 1 -> 0; matrix products, arithmetic and copies ran while one was open for 1% -> 0% of each run, Pallas kernels for 0% -> 0%
where the time goes in v1:
time: 43.7 us; the launch traced here: 43.5 us
  Pallas kernels  40 us (92%)
  local copies, waits for them, and re-layouts  2.85 us (7%)
  between operations  0.64 us (1%)
    pallas_call x1, Pallas kernels, shards(): pl.pallas_call(functools.partial(kernel, freqs, panels, lanes), out_shape...  40 us
    unnamed x2, local copies, waits for them, and re-layouts  2.85 us

profile of v1, /device:TPU:0, one launch (start us, length us, event | category | flops | bytes accessed | tf_op | source)
XLA Modules:
  0.0 43.5 jit_solution(16613272412033572049)
XLA Ops:
  0.6 40.0 %spectra.1 = (f32[64,128]{1,0:T(8,128)}, f32[64,256]{1,0:T(8,128)}) custom-call(bf16[2,128,1024]{2,1,0:T(8,128)(2,1)} %sources_hbm.1, bf16[128,1024]{1,0:T(8,128)(2,1)} %constant.4.clone.dft_hbm, f32[3,256]{1,0:T(4,128)} %pos_hbm.1, f32[2,256]{1,0:T(2,128)} %normal_hbm.1, f32[2,2048]{1,0:T(2,128)} %angle_hbm.1, f32[2,2,32,3072]{3,2,1,0:T(8,128)} %constant.5.clone.table_hbm, ...), custom_call_target="tpu_custom_call" | custom-call | tf_op jit(solution)/shard_map/spectra/pallas_call | solution.py:649
  40.6 1.4 %copy.16 = f32[128,64]{0,1:T(8,128)} copy(f32[128,64]{0,1:T(8,128)} %bitcast.8) | data formatting | bytes 65536
  42.0 1.5 %copy.17 = f32[64,256]{1,0:T(8,128)} copy(f32[64,256]{1,0:T(8,128)} %get-tuple-element.9) | data formatting | bytes 131072
